TPU v7x, 32 devices: a whole 2x2x4 slice. The times are simulated.
32 devices in a mesh: tm: 8 (over z, y), lat: 4 (over x, core).
Axes of the slice: x: 2, y: 2, z: 4, core: 2. Of those that a mesh axis runs over, the one named last changes fastest.
Arguments:
- traj: float32 [8, 83, 24, 192], P('tm', None, 'lat'), may hold values from -6 to 6
- noise: float32 [8, 83, 24, 192], P('tm', None, 'lat'), may hold values from -6 to 6
- step_index: int32 [8], P('tm'), may hold values from 0 to 999
- embed_weight: bfloat16 [83, 512], replicated, may hold values from -0.625 to 0.625
- time_weight: float32 [512, 512], replicated, may hold values from -0.25 to 0.25
- dw_weight: float32 [512, 25], replicated, may hold values from -1.25 to 1.25
- ln_gain: float32 [512], replicated, may hold values from 0.5 to 1.5
- up_weight: bfloat16 [512, 1024], replicated, may hold values from -0.25 to 0.25
- down_weight: bfloat16 [1024, 512], replicated, may hold values from -0.1875 to 0.1875
- out_weight: bfloat16 [512, 83], replicated, may hold values from -0.25 to 0.25
Outputs:
- trajectory: float32 [8, 83, 24, 192], P('tm', None, 'lat')
All inputs are finite; a program needn't handle non-finite values.
Results may differ from a plain program's by a relative error of at most 0.0025.
Values may be sent and summed in bfloat16 or wider, within the bound.
No kernel may reach another device: no remote copies, remote signals or barrier semaphores. Data moves between devices by JAX's collectives and lax.ppermute only.
A program may use at most 128 MiB of HBM per device.

v0:
```python
import math
import jax
import jax.numpy as jnp
from jax import lax
from jax.sharding import PartitionSpec as P

ITERS = 2
LEVELS = 1000


def with_halo(x, sides, width):
    for axis, dim in sides:
        devices, length = (lax.axis_size(axis), x.shape[dim])
        up = [(i, (i + 1) % devices) for i in range(devices - 1)]
        down = [(j, i) for i, j in up]
        last = lax.slice_in_dim(x, length - width, length, axis=dim)
        first = lax.slice_in_dim(x, 0, width, axis=dim)
        before = lax.ppermute(last, axis, up)
        after = lax.ppermute(first, axis, down)
        x = jnp.concatenate([before, x, after], axis=dim)
    return x


def entering(part, axis, combine, identity):
    place = lax.axis_index(axis)
    gathered = lax.all_gather(part, axis)
    state = jnp.zeros_like(part) + jnp.asarray(identity, part.dtype)

    def one(turn, state):
        return combine(state, lax.dynamic_index_in_dim(gathered, turn, 0, False))

    return lax.fori_loop(0, place, one, state)


def spread(value, axis, source):
    kept = jnp.where(lax.axis_index(axis) == source, value, 0).astype(value.dtype)
    return lax.psum(kept, axis)


def noise_levels(step_index):
    log_ratio = math.log(0.1) / (LEVELS - 1)
    return 2.0 * jnp.exp(step_index.astype(jnp.float32) * log_ratio)


def conditions(noise_level, time_weight):
    half_width = time_weight.shape[0] // 2
    frequency = jnp.exp(jnp.arange(half_width, dtype=jnp.float32) * (-math.log(100.0) / half_width))
    angles = jnp.log(noise_level)[:, None] * frequency[None, :]
    features = jnp.concatenate([jnp.cos(angles), jnp.sin(angles)], axis=1)
    return jax.nn.silu(jnp.dot(features, time_weight, precision=lax.Precision.HIGHEST))


def depthwise_taps(lat_padded, dw_weight):
    lat_rows = lat_padded.shape[1] - 4
    widened = lat_padded.astype(jnp.float32)
    lon_cols = widened.shape[2]
    widened = jnp.concatenate([widened[:, :, -2:], widened, widened[:, :, :2]], axis=2)
    summed = jnp.zeros((widened.shape[0], lat_rows, lon_cols), jnp.float32)
    for row_tap in range(5):
        for col_tap in range(5):
            summed = (
                summed
                + dw_weight[:, row_tap * 5 + col_tap][:, None, None]
                * widened[:, row_tap : row_tap + lat_rows, col_tap : col_tap + lon_cols]
            )
    return summed


def denoise(
    current, condition, embed_weight, dw_weight, ln_gain, up_weight, down_weight, out_weight
):
    channels, lat_rows, lon_cols = current.shape
    width = embed_weight.shape[1]
    as_rows = current.astype(jnp.bfloat16).reshape(channels, lat_rows * lon_cols)
    embedded = jnp.dot(embed_weight.T, as_rows, preferred_element_type=jnp.float32)
    activation = (embedded + condition[:, None]).astype(jnp.bfloat16)
    padded = with_halo(activation.reshape(width, lat_rows, lon_cols), (("lat", 1),), 2)
    convolved = depthwise_taps(padded, dw_weight).reshape(width, lat_rows * lon_cols)
    average = jnp.mean(convolved, axis=0)
    centred = convolved - average[None, :]
    variance = jnp.mean(centred * centred, axis=0)
    normed = (centred * lax.rsqrt(variance + 1e-06)[None, :] * ln_gain[:, None]).astype(
        jnp.bfloat16
    )
    hidden = jax.nn.gelu(
        jnp.dot(up_weight.T, normed, preferred_element_type=jnp.float32), approximate=True
    ).astype(jnp.bfloat16)
    block_out = (
        activation.astype(jnp.float32)
        + jnp.dot(down_weight.T, hidden, preferred_element_type=jnp.float32)
    ).astype(jnp.bfloat16)
    return jnp.dot(out_weight.T, block_out, preferred_element_type=jnp.float32).reshape(
        channels, lat_rows, lon_cols
    )


def add_terms(earlier, later):
    return earlier + later


def earlier_sum(increment):
    return entering(increment, "tm", add_terms, jnp.zeros_like(increment))


def shards(
    traj,
    noise,
    step_index,
    embed_weight,
    time_weight,
    dw_weight,
    ln_gain,
    up_weight,
    down_weight,
    out_weight,
):
    noise_level = noise_levels(step_index)
    condition = conditions(noise_level, time_weight)[0]
    level_now = noise_level[0]
    root = traj[0]
    anchor = spread(root, "tm", 0)
    current = root
    for picard_step in range(ITERS):
        drift_term = denoise(
            current, condition, embed_weight, dw_weight, ln_gain, up_weight, down_weight, out_weight
        )
        increment = 0.125 * level_now * drift_term + 0.125 * jnp.sqrt(level_now) * noise[0]
        current = anchor + earlier_sum(increment)
    return current[None]


def solution(mesh):
    in_specs = (
        P("tm", None, "lat", None),
        P("tm", None, "lat", None),
        P("tm"),
        P(),
        P(),
        P(),
        P(),
        P(),
        P(),
        P(),
    )
    out_specs = P("tm", None, "lat", None)
    return jax.shard_map(shards, mesh=mesh, in_specs=in_specs, out_specs=out_specs, check_vma=False)
```

profile of v0, /device:TPU:29, one launch (start us, length us, event | category | flops | bytes accessed | tf_op | source)
XLA Modules:
  0.0 318.5 jit_solution(5527043713613700483)
XLA Ops:
  7.4 1.8 fusion.162
  9.3 2.4 convert_reduce_fusion
  12.0 0.5 fusion.22
  12.6 0.6 copy.24
  13.3 3.7 %collective-permute-start = (bf16[512,2,192]{0,2,1:T(8,128)(2,1)S(1)}, bf16[512,2,192]{0,2,1:T(8,128)(2,1)S(1)}, u32[]{:S(2)}, u32[]{:S(2)}) collective-permute-start(bf16[512,2,192]{0,2,1:T(8,128)(2,1)S(1)} %get-tuple-element.87), channel_id=1, source_target_pairs={{0,1},{1,2},{2,3},{4,5},{5,6},{6,7},{8,9},{9,10},{10,11},{12,13},{... | collective-permute-start | bytes 1179656 | tf_op jit(solution)/shard_map/ppermute | solution.py:18
  17.0 1.9 collective-permute-start.1
  18.9 0.9 fusion.177
  19.8 1.2 fusion.176
  21.7 4.4 %collective-permute-done.1 = bf16[512,2,192]{0,2,1:T(8,128)(2,1)S(1)} collective-permute-done((bf16[512,2,192]{0,2,1:T(8,128)(2,1)S(1)}, bf16[512,2,192]{0,2,1:T(8,128)(2,1)S(1)}, u32[]{:S(2)}, u32[]{:S(2)}) %collective-permute-start.1) | collective-permute-done | bytes 393248 | tf_op jit(solution)/shard_map/ppermute | solution.py:19
  26.6 8.8 %fusion.170 = (f32[6,192]{1,0:T(8,128)S(1)}, f32[512,6,192]{0,2,1:T(8,128)S(1)}) fusion(f32[512,10,2]{0,2,1:T(2,128)S(1)} %get-tuple-element.84, f32[512,10,192]{0,2,1:T(8,128)S(1)} %maximum_convert_fusion, f32[512]{0:T(512)S(1)} %bitcast.124, f32[512]{0:T(512)S(1)} %bitcast.126, f32[512]{0:T(512)S(1)} %bitcast.130, ...), kind=kLoop, calls=%fused_computation.285 | loop fusion | flops 41286528 | bytes 18225664 | tf_op jit(solution)/shard_map/reduce_sum | solution.py:79
  35.5 0.5 multiply_reduce_fusion.1
  36.1 1.1 fusion.155
  37.2 3.5 %fusion.9 = bf16[1024,1152]{0,1:T(8,128)(2,1)} fusion(bf16[512,1152]{0,1:T(8,128)(2,1)S(1)} %fusion.155, bf16[512,1024]{1,0:T(8,128)(2,1)S(1)} %copy-done), kind=kOutput, calls=%fused_computation.51 | convolution fusion | flops 1218576384 | bytes 4587520 | tf_op jit(solution)/shard_map/dot_general | solution.py:86
  40.8 4.5 %fusion.24 = f32[83,1152]{1,0:T(8,128)} fusion(bf16[512,83]{0,1:T(8,128)(2,1)S(1)} %copy-done.47, bf16[1024,1152]{0,1:T(8,128)(2,1)} %fusion.9, bf16[1024,512]{1,0:T(8,128)(2,1)} %param.22, bf16[512,1152]{1,0:T(8,128)(2,1)S(1)} %copy-done.4, f32[]{:T(128)} %bitcast.3), kind=kOutput, calls=%fused_computation.108 | convolution fusion | flops 1307735424 | bytes 5054980 | tf_op jit(solution)/shard_map/dot_general | solution.py:92
  45.3 1.3 mul.669
  46.7 1.0 copy.27
  47.8 0.9 fusion.161
  48.7 70.6 %all-gather.3.cloned.1.call-done = f32[8,83,6,192]{3,1,2,0:T(8,128)} async-done(((f32[1,83,6,192]{3,1,2,0:T(8,128)}), f32[8,83,6,192]{3,1,2,0:T(8,128)}) %all-gather.3.cloned.1.call-update) | async-done | bytes 3059728 | tf_op jit(solution)/shard_map/all_gather | solution.py:26
  119.4 9.9 %while.20 = (s32[]{:T(128)}, f32[83,6,192]{2,1,0:T(8,128)S(1)}, s32[]{:T(128)}, f32[8,83,6,192]{3,1,2,0:T(8,128)}, s32[]{:T(128)}, /*index=5*/s32[]{:T(128)}, s32[]{:T(128)}) while((s32[]{:T(128)}, f32[83,6,192]{2,1,0:T(8,128)S(1)}, s32[]{:T(128)}, f32[8,83,6,192]{3,1,2,0:T(8,128)}, s32[]{:T(128)}, /*index=5*/s32[]{:T(128)}, s32[]{:T(128)}) %tuple.63), condition=%wide.region_4.5_spmd, body=%wide.region_3.4_spmd.sunk | while | flops 95621 | bytes 1912435 | solution.py:32
  119.4 1.1 constant_dynamic-slice_fusion.4
  120.8 1.1 constant_dynamic-slice_fusion.4
  122.2 1.1 constant_dynamic-slice_fusion.4
  123.6 1.1 constant_dynamic-slice_fusion.4
  125.0 1.1 constant_dynamic-slice_fusion.4
  126.4 1.1 constant_dynamic-slice_fusion.4
  127.8 1.1 constant_dynamic-slice_fusion.4
  129.4 63.4 %all-reduce.2.cloned.1.call-done = f32[83,6,192]{2,0,1:T(8,128)} async-done(((f32[83,6,192]{2,0,1:T(8,128)}), f32[83,6,192]{2,0,1:T(8,128)}) %all-reduce.2.cloned.1.call-update) | async-done | bytes 382480 | tf_op jit(solution)/shard_map/psum | solution.py:37
  192.7 1.2 fusion.160
  194.3 0.5 fusion.23
  194.9 5.7 %collective-permute-start.2 = (bf16[512,2,192]{0,2,1:T(8,128)(2,1)S(1)}, bf16[512,2,192]{0,2,1:T(8,128)(2,1)S(1)}, u32[]{:S(2)}, u32[]{:S(2)}) collective-permute-start(bf16[512,2,192]{0,2,1:T(8,128)(2,1)S(1)} %get-tuple-element.85), channel_id=1, source_target_pairs={{0,1},{1,2},{2,3},{4,5},{5,6},{6,7},{8,9},{9,10},{10,11},{12,13},{... | collective-permute-start | bytes 1179656 | tf_op jit(solution)/shard_map/ppermute | solution.py:18
  200.7 1.9 collective-permute-start.3
  202.6 2.6 collective-permute-done.2
  205.2 4.6 %collective-permute-done.3 = bf16[512,2,192]{0,2,1:T(8,128)(2,1)S(1)} collective-permute-done((bf16[512,2,192]{0,2,1:T(8,128)(2,1)S(1)}, bf16[512,2,192]{0,2,1:T(8,128)(2,1)S(1)}, u32[]{:S(2)}, u32[]{:S(2)}) %collective-permute-start.3) | collective-permute-done | bytes 393248 | tf_op jit(solution)/shard_map/ppermute | solution.py:19
  210.3 8.8 %fusion.168 = (f32[6,192]{1,0:T(8,128)S(1)}, f32[512,6,192]{0,2,1:T(8,128)S(1)}) fusion(f32[512,10,2]{0,2,1:T(2,128)S(1)} %get-tuple-element.82, f32[512,10,192]{0,2,1:T(8,128)S(1)} %maximum_convert_fusion.1, f32[512]{0:T(512)S(1)} %bitcast.125, f32[512]{0:T(512)S(1)} %bitcast.127, f32[512]{0:T(512)S(1)} %bitcast.131, ...), kind=kLoop, calls=%fused_computation.284 | loop fusion | flops 41286528 | bytes 18225664 | tf_op jit(solution)/shard_map/reduce_sum | solution.py:79
  219.3 0.5 multiply_reduce_fusion
  220.3 3.5 %fusion.17 = bf16[1024,1152]{0,1:T(8,128)(2,1)} fusion(bf16[512,1152]{0,1:T(8,128)(2,1)S(1)} %fusion.152, bf16[512,1024]{1,0:T(8,128)(2,1)S(1)} %copy-done), kind=kOutput, calls=%fused_computation.59 | convolution fusion | flops 1218576384 | bytes 4587520 | tf_op jit(solution)/shard_map/dot_general | solution.py:86
  223.9 3.7 %fusion.25 = f32[83,1152]{1,0:T(8,128)S(1)} fusion(bf16[512,83]{0,1:T(8,128)(2,1)S(1)} %copy-done.48, bf16[1024,1152]{0,1:T(8,128)(2,1)} %fusion.17, bf16[1024,512]{1,0:T(8,128)(2,1)} %param.22, bf16[1152,512]{1,0:T(8,128)(2,1)S(1)} %copy-done.2, f32[]{:T(128)} %bitcast.3), kind=kOutput, calls=%fused_computation.109 | convolution fusion | flops 1307735424 | bytes 5054980 | tf_op jit(solution)/shard_map/dot_general | solution.py:92
  228.0 1.0 copy.31
  229.0 71.6 %all-gather.5.cloned.1.call-done = f32[8,83,6,192]{3,1,2,0:T(8,128)} async-done(((f32[1,83,6,192]{3,1,2,0:T(8,128)}), f32[8,83,6,192]{3,1,2,0:T(8,128)}) %all-gather.5.cloned.1.call-update) | async-done | bytes 3059728 | tf_op jit(solution)/shard_map/all_gather | solution.py:26
  300.7 9.8 %while.21 = (s32[]{:T(128)}, f32[83,6,192]{2,1,0:T(8,128)S(1)}, s32[]{:T(128)}, f32[8,83,6,192]{3,1,2,0:T(8,128)}, s32[]{:T(128)}, /*index=5*/s32[]{:T(128)}, s32[]{:T(128)}) while((s32[]{:T(128)}, f32[83,6,192]{2,1,0:T(8,128)S(1)}, s32[]{:T(128)}, f32[8,83,6,192]{3,1,2,0:T(8,128)}, s32[]{:T(128)}, /*index=5*/s32[]{:T(128)}, s32[]{:T(128)}) %tuple.66), condition=%wide.region_8.9_spmd, body=%wide.region_7.8_spmd.sunk | while | flops 95621 | bytes 1912435 | solution.py:32
  300.7 1.1 constant_dynamic-slice_fusion.5
  302.1 1.1 constant_dynamic-slice_fusion.5
  303.5 1.1 constant_dynamic-slice_fusion.5
  304.9 1.1 constant_dynamic-slice_fusion.5
  306.3 1.1 constant_dynamic-slice_fusion.5
  307.7 1.1 constant_dynamic-slice_fusion.5
  309.1 1.1 constant_dynamic-slice_fusion.5
  310.7 1.3 copy.34
  (145 shorter events, 7.5 us)
Async XLA Ops:
  6.5 30.7 %copy-start = (bf16[512,1024]{1,0:T(8,128)(2,1)S(1)}, bf16[512,1024]{1,0:T(8,128)(2,1)}, u32[]{:S(2)}) copy-start(bf16[512,1024]{1,0:T(8,128)(2,1)} %param.21) | copy-start | bytes 3145732
  6.5 5.5 %copy-start.9 = (bf16[83,512]{1,0:T(8,128)(2,1)S(1)}, bf16[83,512]{1,0:T(8,128)(2,1)}, u32[]{:S(2)}) copy-start(bf16[83,512]{1,0:T(8,128)(2,1)} %param.17) | copy-start | bytes 254980
  6.5 112.8 %all-gather.3.cloned.1.call-start = ((), (), s32[]{:S(2)}) async-start(), calls=%async_computation.1 | async-start | bytes 4866048 | tf_op jit(solution)/shard_map/all_gather | solution.py:26
  12.6 13.8 %copy-start.3 = (bf16[512,1152]{1,0:T(8,128)(2,1)}, bf16[512,1152]{1,0:T(8,128)(2,1)S(1)}, u32[]{:S(2)}) copy-start(bf16[512,1152]{1,0:T(8,128)(2,1)S(1)} %fusion.22) | copy-start | bytes 3538948
  13.3 8.4 %collective-permute-start = (bf16[512,2,192]{0,2,1:T(8,128)(2,1)S(1)}, bf16[512,2,192]{0,2,1:T(8,128)(2,1)S(1)}, u32[]{:S(2)}, u32[]{:S(2)}) collective-permute-start(bf16[512,2,192]{0,2,1:T(8,128)(2,1)S(1)} %get-tuple-element.87), channel_id=1, source_target_pairs={{0,1},{1,2},{2,3},{4,5},{5,6},{6,7},{8,9},{9,10},{10,11},{12,13},{... | collective-permute-start | bytes 1179656 | tf_op jit(solution)/shard_map/ppermute | solution.py:18
  17.0 9.1 %collective-permute-start.1 = (bf16[512,2,192]{0,2,1:T(8,128)(2,1)S(1)}, bf16[512,2,192]{0,2,1:T(8,128)(2,1)S(1)}, u32[]{:S(2)}, u32[]{:S(2)}) collective-permute-start(bf16[512,2,192]{0,2,1:T(8,128)(2,1)S(1)} %get-tuple-element.88), channel_id=1, source_target_pairs={{1,0},{2,1},{3,2},{5,4},{6,5},{7,6},{9,8},{10,9},{11,10},{13,12},{... | collective-permute-start | bytes 1179656 | tf_op jit(solution)/shard_map/ppermute | solution.py:19
  21.0 5.3 %copy-start.10 = (f32[512,1]{0,1:T(1,128)}, f32[512,1]{0,1:T(1,128)S(1)}, u32[]{:S(2)}) copy-start(f32[512,1]{0,1:T(1,128)S(1)} %get-tuple-element.91) | copy-start | bytes 6148
  21.1 5.3 %copy-start.12 = (f32[512,1]{0,1:T(1,128)}, f32[512,1]{0,1:T(1,128)S(1)}, u32[]{:S(2)}) copy-start(f32[512,1]{0,1:T(1,128)S(1)} %get-tuple-element.92) | copy-start | bytes 6148
  21.1 5.3 %copy-start.14 = (f32[512,1]{0,1:T(1,128)}, f32[512,1]{0,1:T(1,128)S(1)}, u32[]{:S(2)}) copy-start(f32[512,1]{0,1:T(1,128)S(1)} %get-tuple-element.93) | copy-start | bytes 6148
  21.1 5.3 %copy-start.16 = (f32[512,1]{0,1:T(1,128)}, f32[512,1]{0,1:T(1,128)S(1)}, u32[]{:S(2)}) copy-start(f32[512,1]{0,1:T(1,128)S(1)} %get-tuple-element.94) | copy-start | bytes 6148
  21.1 5.3 %copy-start.18 = (f32[512,1]{0,1:T(1,128)}, f32[512,1]{0,1:T(1,128)S(1)}, u32[]{:S(2)}) copy-start(f32[512,1]{0,1:T(1,128)S(1)} %get-tuple-element.95) | copy-start | bytes 6148
  21.1 5.3 %copy-start.20 = (f32[512,1]{0,1:T(1,128)}, f32[512,1]{0,1:T(1,128)S(1)}, u32[]{:S(2)}) copy-start(f32[512,1]{0,1:T(1,128)S(1)} %get-tuple-element.96) | copy-start | bytes 6148
  21.1 5.3 %copy-start.22 = (f32[512,1]{0,1:T(1,128)}, f32[512,1]{0,1:T(1,128)S(1)}, u32[]{:S(2)}) copy-start(f32[512,1]{0,1:T(1,128)S(1)} %get-tuple-element.97) | copy-start | bytes 6148
  21.1 5.3 %copy-start.24 = (f32[512,1]{0,1:T(1,128)}, f32[512,1]{0,1:T(1,128)S(1)}, u32[]{:S(2)}) copy-start(f32[512,1]{0,1:T(1,128)S(1)} %get-tuple-element.98) | copy-start | bytes 6148
  21.1 5.3 %copy-start.26 = (f32[512,1]{0,1:T(1,128)}, f32[512,1]{0,1:T(1,128)S(1)}, u32[]{:S(2)}) copy-start(f32[512,1]{0,1:T(1,128)S(1)} %get-tuple-element.99) | copy-start | bytes 6148
  21.1 5.3 %copy-start.28 = (f32[512,1]{0,1:T(1,128)}, f32[512,1]{0,1:T(1,128)S(1)}, u32[]{:S(2)}) copy-start(f32[512,1]{0,1:T(1,128)S(1)} %get-tuple-element.100) | copy-start | bytes 6148
  21.1 5.3 %copy-start.30 = (f32[512,1]{0,1:T(1,128)}, f32[512,1]{0,1:T(1,128)S(1)}, u32[]{:S(2)}) copy-start(f32[512,1]{0,1:T(1,128)S(1)} %get-tuple-element.101) | copy-start | bytes 6148
  21.2 5.3 %copy-start.32 = (f32[512,1]{0,1:T(1,128)}, f32[512,1]{0,1:T(1,128)S(1)}, u32[]{:S(2)}) copy-start(f32[512,1]{0,1:T(1,128)S(1)} %get-tuple-element.102) | copy-start | bytes 6148
  21.2 5.3 %copy-start.34 = (f32[512,1]{0,1:T(1,128)}, f32[512,1]{0,1:T(1,128)S(1)}, u32[]{:S(2)}) copy-start(f32[512,1]{0,1:T(1,128)S(1)} %get-tuple-element.103) | copy-start | bytes 6148
  21.2 5.3 %copy-start.36 = (f32[512,1]{0,1:T(1,128)}, f32[512,1]{0,1:T(1,128)S(1)}, u32[]{:S(2)}) copy-start(f32[512,1]{0,1:T(1,128)S(1)} %get-tuple-element.104) | copy-start | bytes 6148
  21.2 5.3 %copy-start.38 = (f32[512,1]{0,1:T(1,128)}, f32[512,1]{0,1:T(1,128)S(1)}, u32[]{:S(2)}) copy-start(f32[512,1]{0,1:T(1,128)S(1)} %get-tuple-element.105) | copy-start | bytes 6148
  21.2 5.3 %copy-start.40 = (f32[512,1]{0,1:T(1,128)}, f32[512,1]{0,1:T(1,128)S(1)}, u32[]{:S(2)}) copy-start(f32[512,1]{0,1:T(1,128)S(1)} %get-tuple-element.106) | copy-start | bytes 6148
  21.2 5.3 %copy-start.42 = (f32[512,1]{0,1:T(1,128)}, f32[512,1]{0,1:T(1,128)S(1)}, u32[]{:S(2)}) copy-start(f32[512,1]{0,1:T(1,128)S(1)} %get-tuple-element.107) | copy-start | bytes 6148
  40.8 5.8 %copy-start.6 = (f32[1,83,6,192]{3,0,2,1:T(1,128)S(1)}, f32[1,83,6,192]{3,0,2,1:T(1,128)}, u32[]{:S(2)}) copy-start(f32[1,83,6,192]{3,0,2,1:T(1,128)} %param.15) | copy-start | bytes 1147396
  47.7 145.0 %all-reduce.2.cloned.1.call-start = ((), (), s32[]{:S(2)}) async-start(), calls=%async_computation | async-start | bytes 1081344 | tf_op jit(solution)/shard_map/psum | solution.py:37
  48.7 251.9 %all-gather.5.cloned.1.call-start = ((), (), s32[]{:S(2)}) async-start(), calls=%async_computation.2 | async-start | bytes 4866048 | tf_op jit(solution)/shard_map/all_gather | solution.py:26
  129.3 65.0 %copy-start.45 = (f32[512]{0:T(512)S(1)}, f32[512]{0:T(512)}, u32[]{:S(2)}) copy-start(f32[512]{0:T(512)} %copy-done.44) | copy-start | bytes 6148
  194.8 15.3 %copy-start.1 = (bf16[1152,512]{1,0:T(8,128)(2,1)}, bf16[1152,512]{1,0:T(8,128)(2,1)S(1)}, u32[]{:S(2)}) copy-start(bf16[1152,512]{1,0:T(8,128)(2,1)S(1)} %fusion.23) | copy-start | bytes 3538948
  194.9 10.4 %collective-permute-start.2 = (bf16[512,2,192]{0,2,1:T(8,128)(2,1)S(1)}, bf16[512,2,192]{0,2,1:T(8,128)(2,1)S(1)}, u32[]{:S(2)}, u32[]{:S(2)}) collective-permute-start(bf16[512,2,192]{0,2,1:T(8,128)(2,1)S(1)} %get-tuple-element.85), channel_id=1, source_target_pairs={{0,1},{1,2},{2,3},{4,5},{5,6},{6,7},{8,9},{9,10},{10,11},{12,13},{... | collective-permute-start | bytes 1179656 | tf_op jit(solution)/shard_map/ppermute | solution.py:18
  200.5 9.6 %copy-start.11 = (f32[512,1]{0,1:T(1,128)S(1)}, f32[512,1]{0,1:T(1,128)}, u32[]{:S(2)}) copy-start(f32[512,1]{0,1:T(1,128)} %copy-done.10) | copy-start | bytes 6148
  200.6 9.6 %copy-start.13 = (f32[512,1]{0,1:T(1,128)S(1)}, f32[512,1]{0,1:T(1,128)}, u32[]{:S(2)}) copy-start(f32[512,1]{0,1:T(1,128)} %copy-done.12) | copy-start | bytes 6148
  200.6 9.6 %copy-start.15 = (f32[512,1]{0,1:T(1,128)S(1)}, f32[512,1]{0,1:T(1,128)}, u32[]{:S(2)}) copy-start(f32[512,1]{0,1:T(1,128)} %copy-done.14) | copy-start | bytes 6148
  200.6 9.6 %copy-start.17 = (f32[512,1]{0,1:T(1,128)S(1)}, f32[512,1]{0,1:T(1,128)}, u32[]{:S(2)}) copy-start(f32[512,1]{0,1:T(1,128)} %copy-done.16) | copy-start | bytes 6148
  200.6 9.6 %copy-start.19 = (f32[512,1]{0,1:T(1,128)S(1)}, f32[512,1]{0,1:T(1,128)}, u32[]{:S(2)}) copy-start(f32[512,1]{0,1:T(1,128)} %copy-done.18) | copy-start | bytes 6148
  200.6 9.6 %copy-start.21 = (f32[512,1]{0,1:T(1,128)S(1)}, f32[512,1]{0,1:T(1,128)}, u32[]{:S(2)}) copy-start(f32[512,1]{0,1:T(1,128)} %copy-done.20) | copy-start | bytes 6148
  200.6 9.6 %copy-start.23 = (f32[512,1]{0,1:T(1,128)S(1)}, f32[512,1]{0,1:T(1,128)}, u32[]{:S(2)}) copy-start(f32[512,1]{0,1:T(1,128)} %copy-done.22) | copy-start | bytes 6148
  200.6 9.6 %copy-start.25 = (f32[512,1]{0,1:T(1,128)S(1)}, f32[512,1]{0,1:T(1,128)}, u32[]{:S(2)}) copy-start(f32[512,1]{0,1:T(1,128)} %copy-done.24) | copy-start | bytes 6148
  200.6 9.6 %copy-start.27 = (f32[512,1]{0,1:T(1,128)S(1)}, f32[512,1]{0,1:T(1,128)}, u32[]{:S(2)}) copy-start(f32[512,1]{0,1:T(1,128)} %copy-done.26) | copy-start | bytes 6148
  200.6 9.6 %copy-start.29 = (f32[512,1]{0,1:T(1,128)S(1)}, f32[512,1]{0,1:T(1,128)}, u32[]{:S(2)}) copy-start(f32[512,1]{0,1:T(1,128)} %copy-done.28) | copy-start | bytes 6148
  200.6 9.6 %copy-start.31 = (f32[512,1]{0,1:T(1,128)S(1)}, f32[512,1]{0,1:T(1,128)}, u32[]{:S(2)}) copy-start(f32[512,1]{0,1:T(1,128)} %copy-done.30) | copy-start | bytes 6148
  200.7 9.6 %copy-start.33 = (f32[512,1]{0,1:T(1,128)S(1)}, f32[512,1]{0,1:T(1,128)}, u32[]{:S(2)}) copy-start(f32[512,1]{0,1:T(1,128)} %copy-done.32) | copy-start | bytes 6148
  200.7 9.6 %copy-start.35 = (f32[512,1]{0,1:T(1,128)S(1)}, f32[512,1]{0,1:T(1,128)}, u32[]{:S(2)}) copy-start(f32[512,1]{0,1:T(1,128)} %copy-done.34) | copy-start | bytes 6148
  200.7 9.6 %copy-start.37 = (f32[512,1]{0,1:T(1,128)S(1)}, f32[512,1]{0,1:T(1,128)}, u32[]{:S(2)}) copy-start(f32[512,1]{0,1:T(1,128)} %copy-done.36) | copy-start | bytes 6148
  200.7 9.6 %copy-start.39 = (f32[512,1]{0,1:T(1,128)S(1)}, f32[512,1]{0,1:T(1,128)}, u32[]{:S(2)}) copy-start(f32[512,1]{0,1:T(1,128)} %copy-done.38) | copy-start | bytes 6148
  200.7 9.6 %copy-start.41 = (f32[512,1]{0,1:T(1,128)S(1)}, f32[512,1]{0,1:T(1,128)}, u32[]{:S(2)}) copy-start(f32[512,1]{0,1:T(1,128)} %copy-done.40) | copy-start | bytes 6148
  200.7 9.6 %copy-start.43 = (f32[512,1]{0,1:T(1,128)S(1)}, f32[512,1]{0,1:T(1,128)}, u32[]{:S(2)}) copy-start(f32[512,1]{0,1:T(1,128)} %copy-done.42) | copy-start | bytes 6148
  200.7 9.1 %collective-permute-start.3 = (bf16[512,2,192]{0,2,1:T(8,128)(2,1)S(1)}, bf16[512,2,192]{0,2,1:T(8,128)(2,1)S(1)}, u32[]{:S(2)}, u32[]{:S(2)}) collective-permute-start(bf16[512,2,192]{0,2,1:T(8,128)(2,1)S(1)} %get-tuple-element.86), channel_id=1, source_target_pairs={{1,0},{2,1},{3,2},{5,4},{6,5},{7,6},{9,8},{10,9},{11,10},{13,12},{... | collective-permute-start | bytes 1179656 | tf_op jit(solution)/shard_map/ppermute | solution.py:19
  300.6 9.8 %copy-start.5 = (f32[83,6,192]{2,0,1:T(8,128)S(1)}, f32[83,6,192]{2,0,1:T(8,128)}, u32[]{:S(2)}) copy-start(f32[83,6,192]{2,0,1:T(8,128)} %all-reduce.2.cloned.1.call-done) | copy-start | bytes 1147396
  (8 other events, 24.2 us)
Sparse Core Ops, SparseCore 0:
  47.8 71.4 all-gather.2
  122.7 69.9 all-reduce.1
  229.1 71.4 all-gather.4
where the time goes:
time: 320 us; the launch traced here: 319 us
  waiting for transfers between devices  218 us (68%)
  other arithmetic  29.6 us (9%)
  local copies, waits for them, and re-layouts  24.2 us (8%)
  matrix products  18.1 us (6%)
  between operations  14.9 us (5%)
  starting transfers between devices  13.3 us (4%)
    all_gather x2, waiting for transfers between devices, entering(): gathered = lax.all_gather(part, axis)  142 us
    psum x1, waiting for transfers between devices, spread(): return lax.psum(kept, axis)  63.4 us
    reduce_sum x2, other arithmetic, denoise(): average = jnp.mean(convolved, axis=0)  17.7 us
    dynamic_slice x14, local copies, waits for them, and re-layouts, one(): return combine(state, lax.dynamic_index_in_dim(gathered, turn, 0, False))  15.3 us
    ppermute x2, starting transfers between devices, with_halo(): before = lax.ppermute(last, axis, up)  9.34 us
    ppermute x2, waiting for transfers between devices, with_halo(): after = lax.ppermute(first, axis, down)  8.96 us
    dot_general x2, matrix products, denoise(): jnp.dot(out_weight.T, block_out, preferred_element_type=jnp.float32)  8.2 us
    dot_general x2, matrix products, denoise(): jnp.dot(up_weight.T, normed, preferred_element_type=jnp.float32)  7.08 us
  transfers between devices with their start and end apart: 7, of which 7 were waited for; matrix products, arithmetic and copies ran while one was open for 4% of the time, Pallas kernels for 0%

commit v1 on v0

--- a/solution.py
+++ b/solution.py
@@ -3,9 +3,11 @@
 import jax.numpy as jnp
 from jax import lax
 from jax.sharding import PartitionSpec as P
+from jax.lax import all_gather
 
 ITERS = 2
 LEVELS = 1000
+number_skins = lambda in_array, chip_axis: jnp.sum(all_gather(in_array, chip_axis), axis=0)
 
 
 def with_halo(x, sides, width):
@@ -34,7 +36,7 @@
 
 def spread(value, axis, source):
     kept = jnp.where(lax.axis_index(axis) == source, value, 0).astype(value.dtype)
-    return lax.psum(kept, axis)
+    return number_skins(kept, chip_axis=axis)
 
 
 def noise_levels(step_index):

time: 320 us -> 291 us (0.909)
  waiting for transfers between devices: 218 us -> 192 us
    psum x1 -> x0, waiting for transfers between devices: 63.4 us -> none  [spread(): return lax.psum(kept, axis)]
    all_gather x0 -> x1, waiting for transfers between devices: none -> 34.9 us  [all_gather(in_array, chip_axis)]
  transfers between devices with their start and end apart: 7 -> 7, of which waited for: 7 -> 7; matrix products, arithmetic and copies ran while one was open for 4% -> 10% of each run, Pallas kernels for 0% -> 0%
where the time goes in v1:
time: 291 us; the launch traced here: 290 us
  waiting for transfers between devices  192 us (66%)
  other arithmetic  32.4 us (11%)
  local copies, waits for them, and re-layouts  23.3 us (8%)
  matrix products  16.2 us (6%)
  between operations  14.8 us (5%)
  starting transfers between devices  11.3 us (4%)
    all_gather x2, waiting for transfers between devices, entering(): gathered = lax.all_gather(part, axis)  144 us
    all_gather x1, waiting for transfers between devices, all_gather(in_array, chip_axis)  34.9 us
    reduce_sum x2, other arithmetic, denoise(): average = jnp.mean(convolved, axis=0)  17.7 us
    dynamic_slice x14, local copies, waits for them, and re-layouts, one(): return combine(state, lax.dynamic_index_in_dim(gathered, turn, 0, False))  15.3 us
    ppermute x2, waiting for transfers between devices, with_halo(): after = lax.ppermute(first, axis, down)  9.36 us
    dot_general x2, matrix products, denoise(): jnp.dot(out_weight.T, block_out, preferred_element_type=jnp.float32)  7.49 us
    ppermute x2, starting transfers between devices, with_halo(): before = lax.ppermute(last, axis, up)  7.34 us
    dot_general x2, matrix products, denoise(): jnp.dot(up_weight.T, normed, preferred_element_type=jnp.float32)  7.1 us
  transfers between devices with their start and end apart: 7, of which 7 were waited for; matrix products, arithmetic and copies ran while one was open for 10% of the time, Pallas kernels for 0%

profile of v1, /device:TPU:29, one launch (start us, length us, event | category | flops | bytes accessed | tf_op | source)
XLA Modules:
  0.0 290.3 jit_solution(9757228013607176005)
XLA Ops:
  6.6 2.0 copy_select_fusion
  8.7 2.4 convert_reduce_fusion
  11.9 0.6 fusion.161
  13.1 0.5 fusion.22
  13.7 0.6 copy.23
  14.3 3.7 %collective-permute-start = (bf16[512,2,192]{0,2,1:T(8,128)(2,1)S(1)}, bf16[512,2,192]{0,2,1:T(8,128)(2,1)S(1)}, u32[]{:S(2)}, u32[]{:S(2)}) collective-permute-start(bf16[512,2,192]{0,2,1:T(8,128)(2,1)S(1)} %get-tuple-element.87), channel_id=1, source_target_pairs={{0,1},{1,2},{2,3},{4,5},{5,6},{6,7},{8,9},{9,10},{10,11},{12,13},{... | collective-permute-start | bytes 1179656 | tf_op jit(solution)/shard_map/ppermute | solution.py:20
  18.0 1.9 collective-permute-start.1
  20.0 0.9 fusion.176
  20.9 1.2 fusion.175
  22.2 0.5 collective-permute-done
  22.7 4.8 %collective-permute-done.1 = bf16[512,2,192]{0,2,1:T(8,128)(2,1)S(1)} collective-permute-done((bf16[512,2,192]{0,2,1:T(8,128)(2,1)S(1)}, bf16[512,2,192]{0,2,1:T(8,128)(2,1)S(1)}, u32[]{:S(2)}, u32[]{:S(2)}) %collective-permute-start.1) | collective-permute-done | bytes 393248 | tf_op jit(solution)/shard_map/ppermute | solution.py:21
  28.1 8.8 %fusion.169 = (f32[6,192]{1,0:T(8,128)S(1)}, f32[512,6,192]{0,2,1:T(8,128)S(1)}) fusion(f32[512,10,2]{0,2,1:T(2,128)S(1)} %get-tuple-element.84, f32[512,10,192]{0,2,1:T(8,128)S(1)} %maximum_convert_fusion, f32[512]{0:T(512)S(1)} %bitcast.122, f32[512]{0:T(512)S(1)} %bitcast.124, f32[512]{0:T(512)S(1)} %bitcast.128, ...), kind=kLoop, calls=%fused_computation.284 | loop fusion | flops 41286528 | bytes 18225664 | tf_op jit(solution)/shard_map/reduce_sum | solution.py:81
  37.0 0.5 multiply_reduce_fusion.1
  37.6 1.1 fusion.155
  38.7 3.6 %fusion.9 = bf16[1024,1152]{0,1:T(8,128)(2,1)} fusion(bf16[512,1152]{0,1:T(8,128)(2,1)S(1)} %fusion.155, bf16[512,1024]{1,0:T(8,128)(2,1)S(1)} %copy-done), kind=kOutput, calls=%fused_computation.51 | convolution fusion | flops 1218576384 | bytes 4587520 | tf_op jit(solution)/shard_map/dot_general | solution.py:88
  42.3 3.8 %fusion.24 = f32[83,1152]{1,0:T(8,128)S(1)} fusion(bf16[512,83]{0,1:T(8,128)(2,1)S(1)} %copy-done.48, bf16[1024,1152]{0,1:T(8,128)(2,1)} %fusion.9, bf16[1024,512]{1,0:T(8,128)(2,1)} %param.22, bf16[512,1152]{1,0:T(8,128)(2,1)S(1)} %copy-done.6, f32[]{:T(128)} %bitcast.2), kind=kOutput, calls=%fused_computation.108 | convolution fusion | flops 1307735424 | bytes 5054980 | tf_op jit(solution)/shard_map/dot_general | solution.py:94
  46.5 1.0 copy.26
  47.5 34.9 %all-gather.4.cloned.1.call-done = f32[8,83,6,192]{3,1,2,0:T(8,128)} async-done(((f32[1,83,6,192]{3,1,2,0:T(8,128)}), f32[8,83,6,192]{3,1,2,0:T(8,128)}) %all-gather.4.cloned.1.call-update) | async-done | bytes 3059728 | tf_op jit(solution)/shard_map/all_gather | solution.py:10
  82.5 2.6 reduce_sum.45
  85.1 72.5 %all-gather.6.cloned.1.call-done = f32[8,83,6,192]{3,1,2,0:T(8,128)} async-done(((f32[1,83,6,192]{3,1,2,0:T(8,128)}), f32[8,83,6,192]{3,1,2,0:T(8,128)}) %all-gather.6.cloned.1.call-update) | async-done | bytes 3059728 | tf_op jit(solution)/shard_map/all_gather | solution.py:28
  157.6 9.9 %while.20 = (s32[]{:T(128)}, f32[83,6,192]{2,1,0:T(8,128)S(1)}, s32[]{:T(128)}, f32[8,83,6,192]{3,1,2,0:T(8,128)}, s32[]{:T(128)}, /*index=5*/s32[]{:T(128)}, s32[]{:T(128)}) while((s32[]{:T(128)}, f32[83,6,192]{2,1,0:T(8,128)S(1)}, s32[]{:T(128)}, f32[8,83,6,192]{3,1,2,0:T(8,128)}, s32[]{:T(128)}, /*index=5*/s32[]{:T(128)}, s32[]{:T(128)}) %tuple.63), condition=%wide.region_4.5_spmd, body=%wide.region_3.4_spmd.sunk | while | flops 95621 | bytes 1912435 | solution.py:34
  157.7 1.1 constant_dynamic-slice_fusion.4
  159.1 1.1 constant_dynamic-slice_fusion.4
  160.5 1.1 constant_dynamic-slice_fusion.4
  161.9 1.1 constant_dynamic-slice_fusion.4
  163.2 1.1 constant_dynamic-slice_fusion.4
  164.6 1.1 constant_dynamic-slice_fusion.4
  166.0 1.1 constant_dynamic-slice_fusion.4
  168.1 0.5 fusion.23
  168.7 3.7 %collective-permute-start.2 = (bf16[512,2,192]{0,2,1:T(8,128)(2,1)S(1)}, bf16[512,2,192]{0,2,1:T(8,128)(2,1)S(1)}, u32[]{:S(2)}, u32[]{:S(2)}) collective-permute-start(bf16[512,2,192]{0,2,1:T(8,128)(2,1)S(1)} %get-tuple-element.85), channel_id=1, source_target_pairs={{0,1},{1,2},{2,3},{4,5},{5,6},{6,7},{8,9},{9,10},{10,11},{12,13},{... | collective-permute-start | bytes 1179656 | tf_op jit(solution)/shard_map/ppermute | solution.py:20
  172.5 1.9 collective-permute-start.3
  174.5 2.6 collective-permute-done.2
  177.1 4.6 %collective-permute-done.3 = bf16[512,2,192]{0,2,1:T(8,128)(2,1)S(1)} collective-permute-done((bf16[512,2,192]{0,2,1:T(8,128)(2,1)S(1)}, bf16[512,2,192]{0,2,1:T(8,128)(2,1)S(1)}, u32[]{:S(2)}, u32[]{:S(2)}) %collective-permute-start.3) | collective-permute-done | bytes 393248 | tf_op jit(solution)/shard_map/ppermute | solution.py:21
  182.1 8.8 %fusion.167 = (f32[6,192]{1,0:T(8,128)S(1)}, f32[512,6,192]{0,2,1:T(8,128)S(1)}) fusion(f32[512,10,2]{0,2,1:T(2,128)S(1)} %get-tuple-element.82, f32[512,10,192]{0,2,1:T(8,128)S(1)} %maximum_convert_fusion.1, f32[512]{0:T(512)S(1)} %bitcast.123, f32[512]{0:T(512)S(1)} %bitcast.125, f32[512]{0:T(512)S(1)} %bitcast.129, ...), kind=kLoop, calls=%fused_computation.283 | loop fusion | flops 41286528 | bytes 18225664 | tf_op jit(solution)/shard_map/reduce_sum | solution.py:81
  191.1 0.5 multiply_reduce_fusion
  192.1 3.5 %fusion.17 = bf16[1024,1152]{0,1:T(8,128)(2,1)} fusion(bf16[512,1152]{0,1:T(8,128)(2,1)S(1)} %fusion.152, bf16[512,1024]{1,0:T(8,128)(2,1)S(1)} %copy-done), kind=kOutput, calls=%fused_computation.59 | convolution fusion | flops 1218576384 | bytes 4587520 | tf_op jit(solution)/shard_map/dot_general | solution.py:88
  195.6 3.7 %fusion.25 = f32[83,1152]{1,0:T(8,128)S(1)} fusion(bf16[512,83]{0,1:T(8,128)(2,1)S(1)} %copy-done.49, bf16[1024,1152]{0,1:T(8,128)(2,1)} %fusion.17, bf16[1024,512]{1,0:T(8,128)(2,1)} %param.22, bf16[1152,512]{1,0:T(8,128)(2,1)S(1)} %copy-done.2, f32[]{:T(128)} %bitcast.2), kind=kOutput, calls=%fused_computation.109 | convolution fusion | flops 1307735424 | bytes 5054980 | tf_op jit(solution)/shard_map/dot_general | solution.py:94
  199.8 1.0 copy.28
  200.8 71.6 %all-gather.8.cloned.1.call-done = f32[8,83,6,192]{3,1,2,0:T(8,128)} async-done(((f32[1,83,6,192]{3,1,2,0:T(8,128)}), f32[8,83,6,192]{3,1,2,0:T(8,128)}) %all-gather.8.cloned.1.call-update) | async-done | bytes 3059728 | tf_op jit(solution)/shard_map/all_gather | solution.py:28
  272.4 9.8 %while.21 = (s32[]{:T(128)}, f32[83,6,192]{2,1,0:T(8,128)S(1)}, s32[]{:T(128)}, f32[8,83,6,192]{3,1,2,0:T(8,128)}, s32[]{:T(128)}, /*index=5*/s32[]{:T(128)}, s32[]{:T(128)}) while((s32[]{:T(128)}, f32[83,6,192]{2,1,0:T(8,128)S(1)}, s32[]{:T(128)}, f32[8,83,6,192]{3,1,2,0:T(8,128)}, s32[]{:T(128)}, /*index=5*/s32[]{:T(128)}, s32[]{:T(128)}) %tuple.66), condition=%wide.region_8.9_spmd, body=%wide.region_7.8_spmd.sunk | while | flops 95621 | bytes 1912435 | solution.py:34
  272.5 1.1 constant_dynamic-slice_fusion.5
  273.9 1.1 constant_dynamic-slice_fusion.5
  275.3 1.1 constant_dynamic-slice_fusion.5
  276.7 1.1 constant_dynamic-slice_fusion.5
  278.1 1.1 constant_dynamic-slice_fusion.5
  279.5 1.1 constant_dynamic-slice_fusion.5
  280.9 1.1 constant_dynamic-slice_fusion.5
  282.5 1.3 copy.31
  (147 shorter events, 7.8 us)
Async XLA Ops:
  6.5 32.1 %copy-start = (bf16[512,1024]{1,0:T(8,128)(2,1)S(1)}, bf16[512,1024]{1,0:T(8,128)(2,1)}, u32[]{:S(2)}) copy-start(bf16[512,1024]{1,0:T(8,128)(2,1)} %param.21) | copy-start | bytes 3145732
  6.5 6.6 %copy-start.10 = (bf16[83,512]{1,0:T(8,128)(2,1)S(1)}, bf16[83,512]{1,0:T(8,128)(2,1)}, u32[]{:S(2)}) copy-start(bf16[83,512]{1,0:T(8,128)(2,1)} %param.17) | copy-start | bytes 254980
  6.5 75.9 %all-gather.4.cloned.1.call-start = ((), (), s32[]{:S(2)}) async-start(), calls=%async_computation | async-start | bytes 4866048 | tf_op jit(solution)/shard_map/all_gather | solution.py:10
  8.6 149.0 %all-gather.6.cloned.1.call-start = ((), (), s32[]{:S(2)}) async-start(), calls=%async_computation.1 | async-start | bytes 4866048 | tf_op jit(solution)/shard_map/all_gather | solution.py:28
  13.6 14.2 %copy-start.5 = (bf16[512,1152]{1,0:T(8,128)(2,1)}, bf16[512,1152]{1,0:T(8,128)(2,1)S(1)}, u32[]{:S(2)}) copy-start(bf16[512,1152]{1,0:T(8,128)(2,1)S(1)} %fusion.22) | copy-start | bytes 3538948
  14.3 8.4 %collective-permute-start = (bf16[512,2,192]{0,2,1:T(8,128)(2,1)S(1)}, bf16[512,2,192]{0,2,1:T(8,128)(2,1)S(1)}, u32[]{:S(2)}, u32[]{:S(2)}) collective-permute-start(bf16[512,2,192]{0,2,1:T(8,128)(2,1)S(1)} %get-tuple-element.87), channel_id=1, source_target_pairs={{0,1},{1,2},{2,3},{4,5},{5,6},{6,7},{8,9},{9,10},{10,11},{12,13},{... | collective-permute-start | bytes 1179656 | tf_op jit(solution)/shard_map/ppermute | solution.py:20
  18.0 9.5 %collective-permute-start.1 = (bf16[512,2,192]{0,2,1:T(8,128)(2,1)S(1)}, bf16[512,2,192]{0,2,1:T(8,128)(2,1)S(1)}, u32[]{:S(2)}, u32[]{:S(2)}) collective-permute-start(bf16[512,2,192]{0,2,1:T(8,128)(2,1)S(1)} %get-tuple-element.88), channel_id=1, source_target_pairs={{1,0},{2,1},{3,2},{5,4},{6,5},{7,6},{9,8},{10,9},{11,10},{13,12},{... | collective-permute-start | bytes 1179656 | tf_op jit(solution)/shard_map/ppermute | solution.py:21
  22.1 5.8 %copy-start.11 = (f32[512,1]{0,1:T(1,128)}, f32[512,1]{0,1:T(1,128)S(1)}, u32[]{:S(2)}) copy-start(f32[512,1]{0,1:T(1,128)S(1)} %get-tuple-element.91) | copy-start | bytes 6148
  22.1 5.8 %copy-start.13 = (f32[512,1]{0,1:T(1,128)}, f32[512,1]{0,1:T(1,128)S(1)}, u32[]{:S(2)}) copy-start(f32[512,1]{0,1:T(1,128)S(1)} %get-tuple-element.92) | copy-start | bytes 6148
  22.1 5.8 %copy-start.15 = (f32[512,1]{0,1:T(1,128)}, f32[512,1]{0,1:T(1,128)S(1)}, u32[]{:S(2)}) copy-start(f32[512,1]{0,1:T(1,128)S(1)} %get-tuple-element.93) | copy-start | bytes 6148
  22.1 5.8 %copy-start.17 = (f32[512,1]{0,1:T(1,128)}, f32[512,1]{0,1:T(1,128)S(1)}, u32[]{:S(2)}) copy-start(f32[512,1]{0,1:T(1,128)S(1)} %get-tuple-element.94) | copy-start | bytes 6148
  22.1 5.8 %copy-start.19 = (f32[512,1]{0,1:T(1,128)}, f32[512,1]{0,1:T(1,128)S(1)}, u32[]{:S(2)}) copy-start(f32[512,1]{0,1:T(1,128)S(1)} %get-tuple-element.95) | copy-start | bytes 6148
  22.1 5.8 %copy-start.21 = (f32[512,1]{0,1:T(1,128)}, f32[512,1]{0,1:T(1,128)S(1)}, u32[]{:S(2)}) copy-start(f32[512,1]{0,1:T(1,128)S(1)} %get-tuple-element.96) | copy-start | bytes 6148
  22.1 5.8 %copy-start.23 = (f32[512,1]{0,1:T(1,128)}, f32[512,1]{0,1:T(1,128)S(1)}, u32[]{:S(2)}) copy-start(f32[512,1]{0,1:T(1,128)S(1)} %get-tuple-element.97) | copy-start | bytes 6148
  22.1 5.8 %copy-start.25 = (f32[512,1]{0,1:T(1,128)}, f32[512,1]{0,1:T(1,128)S(1)}, u32[]{:S(2)}) copy-start(f32[512,1]{0,1:T(1,128)S(1)} %get-tuple-element.98) | copy-start | bytes 6148
  22.2 5.8 %copy-start.27 = (f32[512,1]{0,1:T(1,128)}, f32[512,1]{0,1:T(1,128)S(1)}, u32[]{:S(2)}) copy-start(f32[512,1]{0,1:T(1,128)S(1)} %get-tuple-element.99) | copy-start | bytes 6148
  22.2 5.8 %copy-start.29 = (f32[512,1]{0,1:T(1,128)}, f32[512,1]{0,1:T(1,128)S(1)}, u32[]{:S(2)}) copy-start(f32[512,1]{0,1:T(1,128)S(1)} %get-tuple-element.100) | copy-start | bytes 6148
  22.2 5.8 %copy-start.31 = (f32[512,1]{0,1:T(1,128)}, f32[512,1]{0,1:T(1,128)S(1)}, u32[]{:S(2)}) copy-start(f32[512,1]{0,1:T(1,128)S(1)} %get-tuple-element.101) | copy-start | bytes 6148
  22.2 5.8 %copy-start.33 = (f32[512,1]{0,1:T(1,128)}, f32[512,1]{0,1:T(1,128)S(1)}, u32[]{:S(2)}) copy-start(f32[512,1]{0,1:T(1,128)S(1)} %get-tuple-element.102) | copy-start | bytes 6148
  22.2 5.8 %copy-start.35 = (f32[512,1]{0,1:T(1,128)}, f32[512,1]{0,1:T(1,128)S(1)}, u32[]{:S(2)}) copy-start(f32[512,1]{0,1:T(1,128)S(1)} %get-tuple-element.103) | copy-start | bytes 6148
  22.2 5.8 %copy-start.37 = (f32[512,1]{0,1:T(1,128)}, f32[512,1]{0,1:T(1,128)S(1)}, u32[]{:S(2)}) copy-start(f32[512,1]{0,1:T(1,128)S(1)} %get-tuple-element.104) | copy-start | bytes 6148
  22.2 5.8 %copy-start.39 = (f32[512,1]{0,1:T(1,128)}, f32[512,1]{0,1:T(1,128)S(1)}, u32[]{:S(2)}) copy-start(f32[512,1]{0,1:T(1,128)S(1)} %get-tuple-element.105) | copy-start | bytes 6148
  22.2 5.8 %copy-start.41 = (f32[512,1]{0,1:T(1,128)}, f32[512,1]{0,1:T(1,128)S(1)}, u32[]{:S(2)}) copy-start(f32[512,1]{0,1:T(1,128)S(1)} %get-tuple-element.106) | copy-start | bytes 6148
  22.2 5.8 %copy-start.43 = (f32[512,1]{0,1:T(1,128)}, f32[512,1]{0,1:T(1,128)S(1)}, u32[]{:S(2)}) copy-start(f32[512,1]{0,1:T(1,128)S(1)} %get-tuple-element.107) | copy-start | bytes 6148
  47.5 224.9 %all-gather.8.cloned.1.call-start = ((), (), s32[]{:S(2)}) async-start(), calls=%async_computation.2 | async-start | bytes 4866048 | tf_op jit(solution)/shard_map/all_gather | solution.py:28
  85.1 82.5 %copy-start.3 = (f32[83,6,192]{2,0,1:T(8,128)}, f32[83,6,192]{2,0,1:T(8,128)S(1)}, u32[]{:S(2)}) copy-start(f32[83,6,192]{2,0,1:T(8,128)S(1)} %reduce_sum.45) | copy-start | bytes 1147396
  157.6 10.5 %copy-start.46 = (f32[512]{0:T(512)S(1)}, f32[512]{0:T(512)}, u32[]{:S(2)}) copy-start(f32[512]{0:T(512)} %copy-done.45) | copy-start | bytes 6148
  168.6 13.3 %copy-start.1 = (bf16[1152,512]{1,0:T(8,128)(2,1)}, bf16[1152,512]{1,0:T(8,128)(2,1)S(1)}, u32[]{:S(2)}) copy-start(bf16[1152,512]{1,0:T(8,128)(2,1)S(1)} %fusion.23) | copy-start | bytes 3538948
  168.7 8.4 %collective-permute-start.2 = (bf16[512,2,192]{0,2,1:T(8,128)(2,1)S(1)}, bf16[512,2,192]{0,2,1:T(8,128)(2,1)S(1)}, u32[]{:S(2)}, u32[]{:S(2)}) collective-permute-start(bf16[512,2,192]{0,2,1:T(8,128)(2,1)S(1)} %get-tuple-element.85), channel_id=1, source_target_pairs={{0,1},{1,2},{2,3},{4,5},{5,6},{6,7},{8,9},{9,10},{10,11},{12,13},{... | collective-permute-start | bytes 1179656 | tf_op jit(solution)/shard_map/ppermute | solution.py:20
  172.4 9.6 %copy-start.12 = (f32[512,1]{0,1:T(1,128)S(1)}, f32[512,1]{0,1:T(1,128)}, u32[]{:S(2)}) copy-start(f32[512,1]{0,1:T(1,128)} %copy-done.11) | copy-start | bytes 6148
  172.4 9.6 %copy-start.14 = (f32[512,1]{0,1:T(1,128)S(1)}, f32[512,1]{0,1:T(1,128)}, u32[]{:S(2)}) copy-start(f32[512,1]{0,1:T(1,128)} %copy-done.13) | copy-start | bytes 6148
  172.4 9.6 %copy-start.16 = (f32[512,1]{0,1:T(1,128)S(1)}, f32[512,1]{0,1:T(1,128)}, u32[]{:S(2)}) copy-start(f32[512,1]{0,1:T(1,128)} %copy-done.15) | copy-start | bytes 6148
  172.4 9.6 %copy-start.18 = (f32[512,1]{0,1:T(1,128)S(1)}, f32[512,1]{0,1:T(1,128)}, u32[]{:S(2)}) copy-start(f32[512,1]{0,1:T(1,128)} %copy-done.17) | copy-start | bytes 6148
  172.4 9.6 %copy-start.20 = (f32[512,1]{0,1:T(1,128)S(1)}, f32[512,1]{0,1:T(1,128)}, u32[]{:S(2)}) copy-start(f32[512,1]{0,1:T(1,128)} %copy-done.19) | copy-start | bytes 6148
  172.4 9.6 %copy-start.22 = (f32[512,1]{0,1:T(1,128)S(1)}, f32[512,1]{0,1:T(1,128)}, u32[]{:S(2)}) copy-start(f32[512,1]{0,1:T(1,128)} %copy-done.21) | copy-start | bytes 6148
  172.4 9.6 %copy-start.24 = (f32[512,1]{0,1:T(1,128)S(1)}, f32[512,1]{0,1:T(1,128)}, u32[]{:S(2)}) copy-start(f32[512,1]{0,1:T(1,128)} %copy-done.23) | copy-start | bytes 6148
  172.4 9.6 %copy-start.26 = (f32[512,1]{0,1:T(1,128)S(1)}, f32[512,1]{0,1:T(1,128)}, u32[]{:S(2)}) copy-start(f32[512,1]{0,1:T(1,128)} %copy-done.25) | copy-start | bytes 6148
  172.4 9.6 %copy-start.28 = (f32[512,1]{0,1:T(1,128)S(1)}, f32[512,1]{0,1:T(1,128)}, u32[]{:S(2)}) copy-start(f32[512,1]{0,1:T(1,128)} %copy-done.27) | copy-start | bytes 6148
  172.4 9.6 %copy-start.30 = (f32[512,1]{0,1:T(1,128)S(1)}, f32[512,1]{0,1:T(1,128)}, u32[]{:S(2)}) copy-start(f32[512,1]{0,1:T(1,128)} %copy-done.29) | copy-start | bytes 6148
  172.5 9.6 %copy-start.32 = (f32[512,1]{0,1:T(1,128)S(1)}, f32[512,1]{0,1:T(1,128)}, u32[]{:S(2)}) copy-start(f32[512,1]{0,1:T(1,128)} %copy-done.31) | copy-start | bytes 6148
  172.5 9.6 %copy-start.34 = (f32[512,1]{0,1:T(1,128)S(1)}, f32[512,1]{0,1:T(1,128)}, u32[]{:S(2)}) copy-start(f32[512,1]{0,1:T(1,128)} %copy-done.33) | copy-start | bytes 6148
  172.5 9.6 %copy-start.36 = (f32[512,1]{0,1:T(1,128)S(1)}, f32[512,1]{0,1:T(1,128)}, u32[]{:S(2)}) copy-start(f32[512,1]{0,1:T(1,128)} %copy-done.35) | copy-start | bytes 6148
  172.5 9.6 %copy-start.38 = (f32[512,1]{0,1:T(1,128)S(1)}, f32[512,1]{0,1:T(1,128)}, u32[]{:S(2)}) copy-start(f32[512,1]{0,1:T(1,128)} %copy-done.37) | copy-start | bytes 6148
  172.5 9.6 %copy-start.40 = (f32[512,1]{0,1:T(1,128)S(1)}, f32[512,1]{0,1:T(1,128)}, u32[]{:S(2)}) copy-start(f32[512,1]{0,1:T(1,128)} %copy-done.39) | copy-start | bytes 6148
  172.5 9.6 %copy-start.42 = (f32[512,1]{0,1:T(1,128)S(1)}, f32[512,1]{0,1:T(1,128)}, u32[]{:S(2)}) copy-start(f32[512,1]{0,1:T(1,128)} %copy-done.41) | copy-start | bytes 6148
  172.5 9.6 %copy-start.44 = (f32[512,1]{0,1:T(1,128)S(1)}, f32[512,1]{0,1:T(1,128)}, u32[]{:S(2)}) copy-start(f32[512,1]{0,1:T(1,128)} %copy-done.43) | copy-start | bytes 6148
  172.5 9.1 %collective-permute-start.3 = (bf16[512,2,192]{0,2,1:T(8,128)(2,1)S(1)}, bf16[512,2,192]{0,2,1:T(8,128)(2,1)S(1)}, u32[]{:S(2)}, u32[]{:S(2)}) collective-permute-start(bf16[512,2,192]{0,2,1:T(8,128)(2,1)S(1)} %get-tuple-element.86), channel_id=1, source_target_pairs={{1,0},{2,1},{3,2},{5,4},{6,5},{7,6},{9,8},{10,9},{11,10},{13,12},{... | collective-permute-start | bytes 1179656 | tf_op jit(solution)/shard_map/ppermute | solution.py:21
  272.4 9.8 %copy-start.4 = (f32[83,6,192]{2,0,1:T(8,128)S(1)}, f32[83,6,192]{2,0,1:T(8,128)}, u32[]{:S(2)}) copy-start(f32[83,6,192]{2,0,1:T(8,128)} %copy-done.3) | copy-start | bytes 1147396
  (9 other events, 29.0 us)
Sparse Core Ops, SparseCore 0:
  9.5 72.9 all-gather.3
  84.7 72.8 all-gather.5
  200.9 71.4 all-gather.7
